TPU v7x, 32 devices: a whole 2x2x4 slice. The times are simulated.
32 devices in a mesh: dp: 2 (over y), row: 4 (over x, core), col: 4 (over z).
Axes of the slice: x: 2, y: 2, z: 4, core: 2. Of those that a mesh axis runs over, the one named last changes fastest.
Arguments:
- tokens: bfloat16 [1024, 1024], P(('dp', 'row'), 'col'), may hold values from -12 to 12
- cotangent: bfloat16 [1024, 1024], P(('dp', 'row'), 'col'), may hold values from -6 to 6
- first_gain: float32 [1024], P('col'), may hold values from 0.25 to 1.75
- first_shift: float32 [1024], P('col'), may hold values from -3 to 3
- w_qkv: bfloat16 [1024, 3072], P('col', 'row'), may hold values from -0.1875 to 0.1875
- bias_qv: float32 [2048], P('row'), may hold values from -4 to 4
- w_out: bfloat16 [1024, 1024], P('row', 'col'), may hold values from -0.375 to 0.375
- bias_out: float32 [1024], P('col'), may hold values from -3 to 3
- second_gain: float32 [1024], P('col'), may hold values from 0.25 to 1.75
- second_shift: float32 [1024], P('col'), may hold values from -3 to 3
- w_up: bfloat16 [1024, 4096], P('col', 'row'), may hold values from -0.1875 to 0.1875
- bias_up: float32 [4096], P('row'), may hold values from -4 to 4
- w_down: bfloat16 [4096, 1024], P('row', 'col'), may hold values from -0.125 to 0.125
- bias_down: float32 [1024], P('col'), may hold values from -3 to 3
Outputs:
- block_out: bfloat16 [1024, 1024], P(('dp', 'row'), 'col')
- grad_tokens: float32 [1024, 1024], P(('dp', 'row'), 'col')
- grad_first_gain: float32 [1024], P('col')
- grad_first_shift: float32 [1024], P('col')
- grad_w_qkv: float32 [1024, 3072], P('col', 'row')
- grad_bias_qv: float32 [2048], P('row')
- grad_w_out: float32 [1024, 1024], P('row', 'col')
- grad_bias_out: float32 [1024], P('col')
- grad_second_gain: float32 [1024], P('col')
- grad_second_shift: float32 [1024], P('col')
- grad_w_up: float32 [1024, 4096], P('col', 'row')
- grad_bias_up: float32 [4096], P('row')
- grad_w_down: float32 [4096, 1024], P('row', 'col')
- grad_bias_down: float32 [1024], P('col')
All inputs are finite; a program needn't handle non-finite values.
Results may differ from a plain program's by a relative error of at most 0.012.
Values may be sent and summed in bfloat16 or wider, within the bound.
No kernel may reach another device: no remote copies, remote signals or barrier semaphores. Data moves between devices by JAX's collectives and lax.ppermute only.
A program may use at most 64 MiB of HBM per device.

v0:
```python
import jax
import jax.numpy as jnp
from jax import lax
from jax.sharding import PartitionSpec as P

HEADS = 16
HEAD_DIM = 64
SEQ = 512
EPS = 1e-05
GELU_C = 0.7978845608028654
GELU_A = 0.044715


def gelu_pair(hidden):
    inner = GELU_C * (hidden + GELU_A * hidden * hidden * hidden)
    tanh_val = jnp.tanh(inner)
    value = 0.5 * hidden * (1.0 + tanh_val)
    slope = 0.5 * (1.0 + tanh_val) + 0.5 * hidden * (1.0 - tanh_val * tanh_val) * GELU_C * (
        1.0 + 3.0 * GELU_A * hidden * hidden
    )
    return (value, slope)


def feature_stats(first_part, second_part):
    return lax.psum((first_part, second_part), "col")


def normalize(matrix, gain, shift):
    width = matrix.shape[1] * lax.axis_size("col")
    total_one, total_two = feature_stats(jnp.sum(matrix, 1), jnp.sum(matrix * matrix, 1))
    centre = total_one / width
    spread = total_two / width - centre * centre
    rstd = lax.rsqrt(spread + EPS)[:, None]
    normed = (matrix - centre[:, None]) * rstd
    return (normed, rstd, (normed * gain + shift).astype(jnp.bfloat16))


def normalize_back(grad, normed, rstd, gain):
    width = grad.shape[1] * lax.axis_size("col")
    scaled = grad * gain
    total_one, total_two = feature_stats(jnp.sum(scaled, 1), jnp.sum(scaled * normed, 1))
    return rstd * (scaled - total_one[:, None] / width - normed * (total_two[:, None] / width))


def product(left, matrix, transposed):
    if transposed:
        return lax.dot_general(
            left, matrix, (((1,), (1,)), ((), ())), preferred_element_type=jnp.float32
        )
    return jnp.dot(left, matrix, preferred_element_type=jnp.float32)


def outer_grad(left, right):
    return lax.dot_general(
        left, right, (((0,), (0,)), ((), ())), preferred_element_type=jnp.float32
    )


def rows_in(block):
    return lax.all_gather(block, "row", axis=0, tiled=True)


def cols_in(block):
    return lax.all_gather(block, "col", axis=0, tiled=True)


def to_cols(whole, matrix, transposed):
    own_rows = whole.shape[0] // lax.axis_size("col")

    def term(first_row, row_count):
        return product(whole, matrix, transposed)

    return lax.psum_scatter(
        term(jnp.int32(0), lax.axis_size("col") * own_rows), "col", scatter_dimension=0, tiled=True
    )


def to_rows(whole, matrix, transposed):
    own_rows = whole.shape[0] // lax.axis_size("row")

    def term(first_row, row_count):
        return product(whole, matrix, transposed)

    return lax.psum_scatter(
        term(jnp.int32(0), lax.axis_size("row") * own_rows), "row", scatter_dimension=0, tiled=True
    )


def block_scores(query_block, query_pos, keys_all, slopes):
    key_pos = jnp.arange(keys_all.shape[0], dtype=jnp.int32)
    offsets = query_pos[:, None] - key_pos[None, :]
    causal_mask = (offsets >= 0) & (query_pos[:, None] // SEQ == key_pos[None, :] // SEQ)
    scores = (
        jnp.einsum("qhe,khe->hqk", query_block, keys_all, preferred_element_type=jnp.float32)
        * 0.125
    )
    scores = scores - slopes[:, None, None] * offsets.astype(jnp.float32)[None]
    return jnp.where(causal_mask[None], scores, -30000.0)


def local(
    tokens,
    cotangent,
    first_gain,
    first_shift,
    w_qkv,
    bias_qv,
    w_out,
    bias_out,
    second_gain,
    second_shift,
    w_up,
    bias_up,
    w_down,
    bias_down,
):
    rows_a = tokens.shape[0]
    group_rows = rows_a * lax.axis_size("row")
    rows_b = group_rows // lax.axis_size("col")
    head_count = bias_qv.shape[0] // (2 * HEAD_DIM)
    head_ids = lax.axis_index("row") * head_count + jnp.arange(head_count, dtype=jnp.int32)
    slopes = jnp.exp2(-8.0 * (head_ids.astype(jnp.float32) + 1.0) / HEADS)
    query_pos = lax.axis_index("col") * rows_b + jnp.arange(rows_b, dtype=jnp.int32)
    block_rows = min(rows_b, 512)
    block_count = rows_b // block_rows
    inputs_f = tokens.astype(jnp.float32)
    normed_one, rstd_one, first_in = normalize(inputs_f, first_gain, first_shift)
    first_all = rows_in(first_in)
    joined = to_cols(first_all, w_qkv, False).reshape(rows_b, head_count, 3, HEAD_DIM)
    bias_pair = bias_qv.reshape(head_count, 2, HEAD_DIM)
    queries = (joined[:, :, 0] + bias_pair[:, 0]).astype(jnp.bfloat16)
    keys_here = joined[:, :, 1].astype(jnp.bfloat16)
    values_here = (joined[:, :, 2] + bias_pair[:, 1]).astype(jnp.bfloat16)
    keys_flat, values_flat = (
        lax.all_gather(keys_here.reshape(rows_b, -1), "col", axis=0, tiled=True),
        lax.all_gather(values_here.reshape(rows_b, -1), "col", axis=0, tiled=True),
    )
    keys_all = keys_flat.reshape(group_rows, head_count, HEAD_DIM)
    values_all = values_flat.reshape(group_rows, head_count, HEAD_DIM)
    query_blocks = queries.reshape(block_count, block_rows, head_count, HEAD_DIM)
    pos_blocks = query_pos.reshape(block_count, block_rows)

    def forward_block(inputs):
        query_block, block_pos = inputs
        scores = block_scores(query_block, block_pos, keys_all, slopes)
        exponent = jnp.exp(scores)
        row_total = jnp.sum(exponent, -1)
        numerator = jnp.einsum(
            "hqk,khe->qhe",
            exponent.astype(jnp.bfloat16),
            values_all,
            preferred_element_type=jnp.float32,
        )
        context_block = (numerator / row_total.T[:, :, None]).astype(jnp.bfloat16)
        return (context_block, jnp.log(row_total))

    context_blocks, logsum_blocks = lax.map(forward_block, (query_blocks, pos_blocks))
    context = context_blocks.reshape(rows_b, head_count * HEAD_DIM)
    context_all = cols_in(context)
    resid = inputs_f + to_rows(context_all, w_out, False) + bias_out
    normed_two, rstd_two, second_in = normalize(resid, second_gain, second_shift)
    second_all = rows_in(second_in)
    pre_act = to_cols(second_all, w_up, False) + bias_up
    act, slope_act = gelu_pair(pre_act)
    act_all = cols_in(act.astype(jnp.bfloat16))
    block_out = (resid + to_rows(act_all, w_down, False) + bias_down).astype(jnp.bfloat16)
    cot_f = cotangent.astype(jnp.float32)
    cot_all = rows_in(cotangent)
    grad_down = outer_grad(act_all, cot_all)
    grad_pre = to_cols(cot_all, w_down, True) * slope_act
    up_bias_part = jnp.sum(grad_pre, 0)
    grad_pre_all = cols_in(grad_pre.astype(jnp.bfloat16))
    grad_up = outer_grad(second_all, grad_pre_all)
    grad_second = to_rows(grad_pre_all, w_up, True)
    second_gain_part = jnp.sum(grad_second * normed_two, 0)
    second_shift_part = jnp.sum(grad_second, 0)
    grad_resid = cot_f + normalize_back(grad_second, normed_two, rstd_two, second_gain)
    out_bias_part = jnp.sum(grad_resid, 0)
    down_bias_part = jnp.sum(cot_f, 0)
    resid_all = rows_in(grad_resid.astype(jnp.bfloat16))
    grad_out = outer_grad(context_all, resid_all)
    grad_context = to_cols(resid_all, w_out, True).astype(jnp.bfloat16)
    grad_ctx_blocks = grad_context.reshape(block_count, block_rows, head_count, HEAD_DIM)

    def backward_block(running, inputs):
        key_acc, value_acc = running
        query_block, block_pos, context_block, grad_block, logsum_block = inputs
        scores = block_scores(query_block, block_pos, keys_all, slopes)
        probs = jnp.exp(scores - logsum_block[:, :, None])
        delta = jnp.sum(grad_block.astype(jnp.float32) * context_block.astype(jnp.float32), -1).T
        dprob = jnp.einsum(
            "qhe,khe->hqk", grad_block, values_all, preferred_element_type=jnp.float32
        )
        dscore = (probs * (dprob - delta[:, :, None])).astype(jnp.bfloat16)
        grad_q = (
            jnp.einsum("hqk,khe->qhe", dscore, keys_all, preferred_element_type=jnp.float32) * 0.125
        )
        key_acc = (
            key_acc
            + jnp.einsum("hqk,qhe->khe", dscore, query_block, preferred_element_type=jnp.float32)
            * 0.125
        )
        value_acc = value_acc + jnp.einsum(
            "hqk,qhe->khe",
            probs.astype(jnp.bfloat16),
            grad_block,
            preferred_element_type=jnp.float32,
        )
        return ((key_acc, value_acc), grad_q)

    empty = jnp.zeros((group_rows, head_count, HEAD_DIM), jnp.float32)
    (key_acc, value_acc), grad_q_blocks = lax.scan(
        backward_block,
        (empty, empty),
        (query_blocks, pos_blocks, context_blocks, grad_ctx_blocks, logsum_blocks),
    )
    grad_k, grad_v = (
        lax.psum_scatter(key_acc.reshape(group_rows, -1), "col", scatter_dimension=0, tiled=True),
        lax.psum_scatter(value_acc.reshape(group_rows, -1), "col", scatter_dimension=0, tiled=True),
    )
    grad_q = grad_q_blocks.reshape(rows_b, head_count, HEAD_DIM)
    grad_k = grad_k.reshape(rows_b, head_count, HEAD_DIM)
    grad_v = grad_v.reshape(rows_b, head_count, HEAD_DIM)
    grad_joined = jnp.stack([grad_q, grad_k, grad_v], 2)
    qv_bias_part = jnp.sum(jnp.stack([grad_q, grad_v], 2), 0).reshape(-1)
    joined_all = cols_in(grad_joined.reshape(rows_b, -1).astype(jnp.bfloat16))
    grad_qkv = outer_grad(first_all, joined_all)
    grad_first = to_rows(joined_all, w_qkv, True)
    first_gain_part = jnp.sum(grad_first * normed_one, 0)
    first_shift_part = jnp.sum(grad_first, 0)
    grad_tokens = grad_resid + normalize_back(grad_first, normed_one, rstd_one, first_gain)
    grad_qkv, grad_out, grad_up, grad_down = lax.psum(
        (grad_qkv, grad_out, grad_up, grad_down), "dp"
    )
    gain_one, shift_one, gain_two, shift_two, out_bias_grad, down_bias_grad = lax.psum(
        (
            first_gain_part,
            first_shift_part,
            second_gain_part,
            second_shift_part,
            out_bias_part,
            down_bias_part,
        ),
        ("dp", "row"),
    )
    qv_bias_grad, up_bias_grad = lax.psum((qv_bias_part, up_bias_part), ("dp", "col"))
    return (
        block_out,
        grad_tokens,
        gain_one,
        shift_one,
        grad_qkv,
        qv_bias_grad,
        grad_out,
        out_bias_grad,
        gain_two,
        shift_two,
        grad_up,
        up_bias_grad,
        grad_down,
        down_bias_grad,
    )


def solution(mesh):
    placed = (
        P(("dp", "row"), "col"),
        P(("dp", "row"), "col"),
        P("col"),
        P("col"),
        P("col", "row"),
        P("row"),
        P("row", "col"),
        P("col"),
        P("col"),
        P("col"),
        P("col", "row"),
        P("row"),
        P("row", "col"),
        P("col"),
    )
    return jax.shard_map(
        local,
        mesh=mesh,
        in_specs=placed,
        out_specs=(
            P(("dp", "row"), "col"),
            P(("dp", "row"), "col"),
            P("col"),
            P("col"),
            P("col", "row"),
            P("row"),
            P("row", "col"),
            P("col"),
            P("col"),
            P("col"),
            P("col", "row"),
            P("row"),
            P("row", "col"),
            P("col"),
        ),
        check_vma=False,
    )
```

profile of v0, /device:TPU:0, one launch (start us, length us, event | category | flops | bytes accessed | tf_op | source)
XLA Modules:
  0.0 548.3 jit_solution(9419298570931146965)
XLA Ops:
  7.2 1.0 convert_reduce_fusion
  8.2 13.5 %all-reduce.5 = (f32[128]{0:T(128)S(1)}, f32[128]{0:T(128)S(1)}) all-reduce(f32[128]{0:T(128)S(1)} %get-tuple-element.85, f32[128]{0:T(128)S(1)} %get-tuple-element.84), channel_id=1, replica_groups=mesh['dp'=2,'row'=4,'col'=4] {'col'}, use_global_device_ids=true, to_apply=%region_3.0 | all-reduce | flops 256 | bytes 2048 | tf_op jit(solution)/shard_map/psum | solution.py:25
  21.7 1.0 fusion.26
  22.7 5.8 %all_gather.30 = bf16[512,256]{1,0:T(8,128)(2,1)S(1)} all-gather(bf16[128,256]{1,0:T(8,128)(2,1)S(1)} %fusion.26), channel_id=1, replica_groups=mesh['dp'=2,'row'=4,'col'=4] {'row'}, dimensions={0}, use_global_device_ids=true | all-gather | bytes 327680 | tf_op jit(solution)/shard_map/all_gather | solution.py:60
  28.5 0.7 copy-done.3
  29.2 2.5 fusion.49
  32.3 33.3 %reduce-scatter.11.cloned.1.call-done = f32[128,768]{1,0:T(8,128)} async-done(((f32[512,768]{1,0:T(8,128)}), f32[128,768]{1,0:T(8,128)}) %reduce-scatter.11.cloned.1.call-update) | async-done | bytes 393232 | tf_op jit(solution)/shard_map/reduce_scatter | solution.py:73
  65.6 1.1 copy.38
  66.9 13.4 %all_gather.31 = bf16[512,256]{0,1:T(8,128)(2,1)S(1)} all-gather(bf16[128,256]{0,1:T(8,128)(2,1)S(1)} %fusion.36), channel_id=1, replica_groups=mesh['dp'=2,'row'=4,'col'=4] {'col'}, dimensions={0}, use_global_device_ids=true | all-gather | bytes 327680 | tf_op jit(solution)/shard_map/all_gather | solution.py:136
  80.2 13.2 %all_gather.32 = bf16[512,256]{0,1:T(8,128)(2,1)S(1)} all-gather(bf16[128,256]{0,1:T(8,128)(2,1)S(1)} %bitcast.91), channel_id=1, replica_groups=mesh['dp'=2,'row'=4,'col'=4] {'col'}, dimensions={0}, use_global_device_ids=true | all-gather | bytes 327680 | tf_op jit(solution)/shard_map/all_gather | solution.py:135
  93.5 0.7 exponential_reduce_fusion
  94.5 12.8 %all_gather.33 = bf16[512,256]{0,1:T(8,128)(2,1)S(1)} all-gather(bf16[128,256]{0,1:T(8,128)(2,1)S(1)} %bitcast.89), channel_id=1, replica_groups=mesh['dp'=2,'row'=4,'col'=4] {'col'}, dimensions={0}, use_global_device_ids=true | all-gather | bytes 327680 | tf_op jit(solution)/shard_map/all_gather | solution.py:64
  107.3 0.7 copy-done.5
  108.0 1.1 fusion.50
  109.1 5.8 %all_gather.36 = bf16[512,256]{1,0:T(8,128)(2,1)S(1)} all-gather(bf16[128,256]{1,0:T(8,128)(2,1)S(1)} %copy-done.21), channel_id=1, replica_groups=mesh['dp'=2,'row'=4,'col'=4] {'row'}, dimensions={0}, use_global_device_ids=true | all-gather | bytes 327680 | tf_op jit(solution)/shard_map/all_gather | solution.py:60
  114.9 0.7 copy-done.9
  115.7 1.8 fusion.53
  117.6 11.7 %reduce-scatter.13.cloned.1.call-done = f32[128,256]{1,0:T(8,128)} async-done(((f32[512,256]{1,0:T(8,128)}), f32[128,256]{1,0:T(8,128)}) %reduce-scatter.13.cloned.1.call-update) | async-done | bytes 131088 | tf_op jit(solution)/shard_map/reduce_scatter | solution.py:84
  129.2 1.0 fusion.42
  130.2 11.8 %all-reduce.4 = (f32[128]{0:T(128)S(1)}, f32[128]{0:T(128)S(1)}) all-reduce(f32[128]{0:T(128)S(1)} %get-tuple-element.83, f32[128]{0:T(128)S(1)} %get-tuple-element.82), channel_id=1, replica_groups=mesh['dp'=2,'row'=4,'col'=4] {'col'}, use_global_device_ids=true, to_apply=%region_10.11 | all-reduce | flops 256 | bytes 2048 | tf_op jit(solution)/shard_map/psum | solution.py:25
  142.2 5.8 %all_gather.34 = bf16[512,256]{1,0:T(8,128)(2,1)S(1)} all-gather(bf16[128,256]{1,0:T(8,128)(2,1)S(1)} %add_convert_fusion.1), channel_id=1, replica_groups=mesh['dp'=2,'row'=4,'col'=4] {'row'}, dimensions={0}, use_global_device_ids=true | all-gather | bytes 327680 | tf_op jit(solution)/shard_map/all_gather | solution.py:60
  148.0 0.7 copy-done.11
  148.7 1.7 fusion.51
  150.5 24.8 %reduce-scatter.19.cloned.1.call-done = f32[128,1024]{1,0:T(8,128)} async-done(((f32[512,1024]{1,0:T(8,128)}), f32[128,1024]{1,0:T(8,128)}) %reduce-scatter.19.cloned.1.call-update) | async-done | bytes 524304 | tf_op jit(solution)/shard_map/reduce_scatter | solution.py:73
  175.2 44.9 %reduce-scatter.15.cloned.1.call-done = f32[128,1024]{1,0:T(8,128)} async-done(((f32[512,1024]{1,0:T(8,128)}), f32[128,1024]{1,0:T(8,128)}) %reduce-scatter.15.cloned.1.call-update) | async-done | bytes 524304 | tf_op jit(solution)/shard_map/reduce_scatter | solution.py:73
  220.1 2.4 fusion.43
  222.6 0.5 all-gather.3.cloned.1.call-update
  223.2 26.7 %all-gather.5.cloned.1.call-done = bf16[512,1024]{1,0:T(8,128)(2,1)} async-done(((bf16[128,1024]{1,0:T(8,128)(2,1)}), bf16[512,1024]{1,0:T(8,128)(2,1)}) %all-gather.5.cloned.1.call-update) | async-done | bytes 1048592 | tf_op jit(solution)/shard_map/all_gather | solution.py:64
  249.9 2.5 fusion.54
  252.5 26.8 %all-gather.3.cloned.1.call-done = bf16[512,1024]{1,0:T(8,128)(2,1)} async-done(((bf16[128,1024]{1,0:T(8,128)(2,1)}), bf16[512,1024]{1,0:T(8,128)(2,1)}) %all-gather.3.cloned.1.call-update) | async-done | bytes 1048592 | tf_op jit(solution)/shard_map/all_gather | solution.py:64
  279.3 2.5 fusion.52
  281.8 21.6 %reduce-scatter.21.cloned.1.call-done = f32[128,256]{1,0:T(8,128)} async-done(((f32[512,256]{1,0:T(8,128)}), f32[128,256]{1,0:T(8,128)}) %reduce-scatter.21.cloned.1.call-update) | async-done | bytes 131088 | tf_op jit(solution)/shard_map/reduce_scatter | solution.py:84
  303.4 1.1 multiply_reduce_fusion
  304.5 11.7 %all-reduce.3 = (f32[128]{0:T(128)S(1)}, f32[128]{0:T(128)S(1)}) all-reduce(f32[128]{0:T(128)S(1)} %get-tuple-element.63, f32[128]{0:T(128)S(1)} %get-tuple-element.67), channel_id=1, replica_groups=mesh['dp'=2,'row'=4,'col'=4] {'col'}, use_global_device_ids=true, to_apply=%region_18.19 | all-reduce | flops 256 | bytes 2048 | tf_op jit(solution)/shard_map/psum | solution.py:25
  316.2 12.0 %reduce-scatter.17.cloned.1.call-done = f32[128,256]{1,0:T(8,128)} async-done(((f32[512,256]{1,0:T(8,128)}), f32[128,256]{1,0:T(8,128)}) %reduce-scatter.17.cloned.1.call-update) | async-done | bytes 131088 | tf_op jit(solution)/shard_map/reduce_scatter | solution.py:84
  328.1 1.6 fusion.45
  329.8 5.8 %all_gather.38 = bf16[512,256]{1,0:T(8,128)(2,1)S(1)} all-gather(bf16[128,256]{1,0:T(8,128)(2,1)S(1)} %convert_element_type.98), channel_id=1, replica_groups=mesh['dp'=2,'row'=4,'col'=4] {'row'}, dimensions={0}, use_global_device_ids=true | all-gather | bytes 327680 | tf_op jit(solution)/shard_map/all_gather | solution.py:60
  335.6 0.7 copy-done.7
  336.3 1.1 fusion.55
  337.4 21.9 %reduce-scatter.23.cloned.1.call-done = f32[128,256]{1,0:T(8,128)} async-done(((f32[512,256]{1,0:T(8,128)}), f32[128,256]{1,0:T(8,128)}) %reduce-scatter.23.cloned.1.call-update) | async-done | bytes 131088 | tf_op jit(solution)/shard_map/reduce_scatter | solution.py:73
  359.3 0.9 convert_element_type.99
  360.3 1.2 fusion.14
  362.0 1.1 convolution_multiply_fusion.1
  363.2 0.9 fusion.48
  364.1 18.0 %reduce-scatter.27.cloned.1.call-done = f32[128,256]{0,1:T(8,128)} async-done(((f32[512,256]{0,1:T(8,128)}), f32[128,256]{0,1:T(8,128)}) %reduce-scatter.27.cloned.1.call-update) | async-done | bytes 131088 | tf_op jit(solution)/shard_map/reduce_scatter | solution.py:219
  382.1 0.9 bitcast_convert_fusion
  383.0 22.0 %reduce-scatter.25.cloned.1.call-done = f32[128,256]{0,1:T(8,128)} async-done(((f32[512,256]{0,1:T(8,128)}), f32[128,256]{0,1:T(8,128)}) %reduce-scatter.25.cloned.1.call-update) | async-done | bytes 131088 | tf_op jit(solution)/shard_map/reduce_scatter | solution.py:218
  405.0 0.9 convert.15
  405.9 17.0 %all_gather.39 = bf16[512,768]{0,1:T(8,128)(2,1)S(1)} all-gather(bf16[128,768]{0,1:T(8,128)(2,1)S(1)} %bitcast.88), channel_id=1, replica_groups=mesh['dp'=2,'row'=4,'col'=4] {'col'}, dimensions={0}, use_global_device_ids=true | all-gather | bytes 983040 | tf_op jit(solution)/shard_map/all_gather | solution.py:64
  422.9 2.3 fusion.56
  425.3 2.4 fusion.59
  427.8 1.4 fusion.60
  429.3 0.9 fusion.58
  430.2 1.3 fusion.57
  431.8 20.6 %all-reduce = (f32[512]{0:T(512)}, f32[1024]{0:T(1024)}) all-reduce(f32[512]{0:T(512)S(1)} %reshape.258, f32[1024]{0:T(1024)S(1)} %get-tuple-element.106), channel_id=1, replica_groups=mesh['dp'=2,'row'=4,'col'=4] {'dp','col'}, use_global_device_ids=true, to_apply=%region_34.35 | all-reduce | flops 1536 | bytes 12288 | tf_op jit(solution)/shard_map/psum | solution.py:246
  452.3 1.1 fusion.31
  453.4 8.4 %all-reduce.2 = (f32[128]{0:T(128)S(1)}, f32[128]{0:T(128)S(1)}) all-reduce(f32[128]{0:T(128)S(1)} %get-tuple-element.65, f32[128]{0:T(128)S(1)} %get-tuple-element.66), channel_id=1, replica_groups=mesh['dp'=2,'row'=4,'col'=4] {'col'}, use_global_device_ids=true, to_apply=%region_27.28 | all-reduce | flops 256 | bytes 2048 | tf_op jit(solution)/shard_map/psum | solution.py:25
  461.8 13.0 %all-reduce.1 = (f32[256]{0:T(256)}, f32[256]{0:T(256)}, f32[256]{0:T(256)}, f32[256]{0:T(256)}, f32[256]{0:T(256)}, /*index=5*/f32[256]{0:T(256)}) all-reduce(f32[256]{0:T(256)S(1)} %get-tuple-element.64, f32[256]{0:T(256)S(1)} %get-tuple-element.81, ...), channel_id=1, replica_groups=mesh['dp'=2,'row'=4,'col'=4] {'dp','row'}, use_global_device_ids=true, to_apply=%region_29.30 | all-reduce | flops 1536 | bytes 12288 | tf_op jit(solution)/shard_map/psum | solution.py:235
  474.8 1.7 fusion.30
  476.5 59.5 %all-reduce.9.cloned.1.call-done = (f32[256,768]{1,0:T(8,128)}, f32[256,256]{1,0:T(8,128)}, f32[256,1024]{1,0:T(8,128)}, f32[1024,256]{1,0:T(8,128)}) async-done(((f32[256,768]{1,0:T(8,128)}, f32[256,256]{1,0:T(8,128)}, f32[256,1024]{1,0:T(8,128)}, f32[1024,256]{1,0:T(8,128)}), (f32[256,768]{1,0:T(8,128)}, f32[256,256]{1,0:T(8,128)}, f32[256,1024]{1,0:T(8,128)}, ...) | async-done | bytes 3145744 | tf_op jit(solution)/shard_map/psum | solution.py:232
  536.0 2.2 copy.46
  538.2 1.7 copy.47
  539.9 1.0 copy.48
  540.8 1.0 copy.49
  (108 shorter events, 2.7 us)
Async XLA Ops:
  7.2 141.5 %copy-start = (bf16[256,1024]{1,0:T(8,128)(2,1)S(1)}, bf16[256,1024]{1,0:T(8,128)(2,1)}, u32[]{:S(2)}) copy-start(bf16[256,1024]{1,0:T(8,128)(2,1)} %param.24) | copy-start | bytes 1572868
  7.2 58.4 %reduce-scatter.11.cloned.1.call-start = ((), (), s32[]{:S(2)}) async-start(), calls=%async_computation.10 | async-start | bytes 1966080 | tf_op jit(solution)/shard_map/reduce_scatter | solution.py:73
  22.7 9.1 %copy-start.25 = (f32[512]{0:T(512)S(1)}, f32[512]{0:T(512)}, u32[]{:S(2)}) copy-start(f32[512]{0:T(512)} %param.19) | copy-start | bytes 6148
  28.5 0.7 copy-start.3
  31.8 97.5 %reduce-scatter.13.cloned.1.call-start = ((), (), s32[]{:S(2)}) async-start(), calls=%async_computation.11 | async-start | bytes 655360 | tf_op jit(solution)/shard_map/reduce_scatter | solution.py:84
  80.2 27.8 %copy-start.18 = (bf16[256,256]{1,0:T(8,128)(2,1)S(1)}, bf16[256,256]{1,0:T(8,128)(2,1)}, u32[]{:S(2)}) copy-start(bf16[256,256]{1,0:T(8,128)(2,1)} %param.20) | copy-start | bytes 393220
  94.2 15.0 %copy-start.21 = (bf16[128,256]{1,0:T(8,128)(2,1)S(1)}, bf16[128,256]{1,0:T(8,128)(2,1)}, u32[]{:S(2)}) copy-start(bf16[128,256]{1,0:T(8,128)(2,1)} %param.15) | copy-start | bytes 196612
  94.2 21.5 %copy-start.12 = (bf16[1024,256]{1,0:T(8,128)(2,1)S(1)}, bf16[1024,256]{1,0:T(8,128)(2,1)}, u32[]{:S(2)}) copy-start(bf16[1024,256]{1,0:T(8,128)(2,1)} %param.26) | copy-start | bytes 1572868
  107.3 0.7 copy-start.5
  109.1 66.1 %reduce-scatter.19.cloned.1.call-start = ((), (), s32[]{:S(2)}) async-start(), calls=%async_computation.15 | async-start | bytes 2621440 | tf_op jit(solution)/shard_map/reduce_scatter | solution.py:73
  114.9 0.7 copy-start.9
  115.6 13.6 %copy-start.13 = (bf16[128,256]{1,0:T(8,128)(2,1)S(1)}, bf16[128,256]{1,0:T(8,128)(2,1)}, u32[]{:S(2)}) copy-start(bf16[128,256]{1,0:T(8,128)(2,1)} %param.14) | copy-start | bytes 196612
  115.6 13.6 %copy-start.26 = (f32[256]{0:T(256)S(1)}, f32[256]{0:T(256)}, u32[]{:S(2)}) copy-start(f32[256]{0:T(256)} %param.21) | copy-start | bytes 3076
  115.6 26.4 %copy-start.22 = (f32[256]{0:T(256)S(1)}, f32[256]{0:T(256)}, u32[]{:S(2)}) copy-start(f32[256]{0:T(256)} %param.22) | copy-start | bytes 3076
  115.6 26.4 %copy-start.27 = (f32[256]{0:T(256)S(1)}, f32[256]{0:T(256)}, u32[]{:S(2)}) copy-start(f32[256]{0:T(256)} %param.23) | copy-start | bytes 3076
  117.5 102.6 %reduce-scatter.15.cloned.1.call-start = ((), (), s32[]{:S(2)}) async-start(), calls=%async_computation.12 | async-start | bytes 2621440 | tf_op jit(solution)/shard_map/reduce_scatter | solution.py:73
  148.0 0.7 copy-start.11
  148.7 71.5 %copy-start.24 = (f32[1024]{0:T(1024)S(1)}, f32[1024]{0:T(1024)}, u32[]{:S(2)}) copy-start(f32[1024]{0:T(1024)} %param.25) | copy-start | bytes 12292
  150.4 99.5 %all-gather.5.cloned.1.call-start = ((), (), s32[]{:S(2)}) async-start(), calls=%async_computation.16 | async-start | bytes 1310720 | tf_op jit(solution)/shard_map/all_gather | solution.py:64
  222.5 56.7 %all-gather.3.cloned.1.call-start = ((), (), s32[]{:S(2)}) async-start(), calls=%async_computation.13 | async-start | bytes 1310720 | tf_op jit(solution)/shard_map/all_gather | solution.py:64
  223.1 80.2 %reduce-scatter.21.cloned.1.call-start = ((), (), s32[]{:S(2)}) async-start(), calls=%async_computation.17 | async-start | bytes 655360 | tf_op jit(solution)/shard_map/reduce_scatter | solution.py:84
  252.4 75.7 %copy-start.28 = (f32[256]{0:T(256)S(1)}, f32[256]{0:T(256)}, u32[]{:S(2)}) copy-start(f32[256]{0:T(256)} %param.27) | copy-start | bytes 3076
  252.4 75.7 %reduce-scatter.17.cloned.1.call-start = ((), (), s32[]{:S(2)}) async-start(), calls=%async_computation.14 | async-start | bytes 655360 | tf_op jit(solution)/shard_map/reduce_scatter | solution.py:84
  281.8 77.6 %reduce-scatter.23.cloned.1.call-start = ((), (), s32[]{:S(2)}) async-start(), calls=%async_computation.18 | async-start | bytes 655360 | tf_op jit(solution)/shard_map/reduce_scatter | solution.py:73
  329.8 31.8 %copy-start.14 = (f32[128,256]{1,0:T(8,128)}, f32[128,256]{1,0:T(8,128)S(1)}, u32[]{:S(2)}) copy-start(f32[128,256]{1,0:T(8,128)S(1)} %get-tuple-element.109) | copy-start | bytes 393220
  335.5 0.7 copy-start.7
  337.3 44.7 %reduce-scatter.27.cloned.1.call-start = ((), (), s32[]{:S(2)}) async-start(), calls=%async_computation.20 | async-start | bytes 655360 | tf_op jit(solution)/shard_map/reduce_scatter | solution.py:219
  361.5 43.4 %reduce-scatter.25.cloned.1.call-start = ((), (), s32[]{:S(2)}) async-start(), calls=%async_computation.19 | async-start | bytes 655360 | tf_op jit(solution)/shard_map/reduce_scatter | solution.py:218
  363.1 89.2 %reduce-scatter.29.cloned.1.call-start = ((), (), s32[]{:S(2)}) async-start(), calls=%async_computation.21 | async-start | bytes 655360 | tf_op jit(solution)/shard_map/reduce_scatter | solution.py:84
  383.0 42.3 %copy-start.1 = (bf16[512,1024]{1,0:T(8,128)(2,1)S(1)}, bf16[512,1024]{1,0:T(8,128)(2,1)}, u32[]{:S(2)}) copy-start(bf16[512,1024]{1,0:T(8,128)(2,1)} %all-gather.5.cloned.1.call-done) | copy-start | bytes 3145732
  422.9 4.9 copy-start.2
  425.3 110.7 %all-reduce.9.cloned.1.call-start = ((), (), s32[]{:S(2)}) async-start(), calls=%async_computation.22 | async-start | bytes 6291456 | tf_op jit(solution)/shard_map/psum | solution.py:232
  425.3 2.5 copy-start.10
  425.3 3.9 copy-start.6
  425.3 3.9 copy-start.8
  427.8 2.4 copy-start.4
  430.2 1.3 copy-start.19
  430.2 1.3 copy-start.20
  431.5 20.9 %copy-start.23 = (f32[256]{0:T(256)S(1)}, f32[256]{0:T(256)}, u32[]{:S(2)}) copy-start(f32[256]{0:T(256)} %param.16) | copy-start | bytes 3076
  431.5 43.3 %copy-start.15 = (f32[128,256]{1,0:T(8,128)S(1)}, f32[128,256]{1,0:T(8,128)}, u32[]{:S(2)}) copy-start(f32[128,256]{1,0:T(8,128)} %copy-done.14) | copy-start | bytes 393220
  536.0 3.9 copy-start.17
  536.0 4.9 copy-start.16
Sparse Core Ops, SparseCore 0:
  31.9 33.6 reduce-scatter.10
  109.2 19.9 reduce-scatter.12
  131.5 43.6 reduce-scatter.18
  177.4 42.6 reduce-scatter.14
  222.7 27.1 all-gather.4
  251.9 27.3 all-gather.2
  282.3 20.9 reduce-scatter.20
  306.4 21.6 reduce-scatter.16
  337.5 21.8 reduce-scatter.22
  362.0 20.0 reduce-scatter.26
  384.9 20.0 reduce-scatter.24
  425.4 20.7 reduce-scatter.28
  449.8 86.1 all-reduce.8
where the time goes:
time: 549 us; the launch traced here: 548 us
  waiting for transfers between devices  324 us (59%)
  blocking collectives  158 us (29%)
  matrix products  26.1 us (5%)
  other arithmetic  14.3 us (3%)
  between operations  14.2 us (3%)
  local copies, waits for them, and re-layouts  11 us (2%)
    reduce_scatter x4, waiting for transfers between devices, to_cols(): lax.psum_scatter(term(jnp.int32(0), lax.axis_size('col') * own_rows), 'co...  125 us
    psum x1, waiting for transfers between devices, local(): lax.psum((grad_qkv, grad_out, grad_up, grad_down), 'dp')  59.5 us
    all_gather x2, waiting for transfers between devices, cols_in(): return lax.all_gather(block, 'col', axis=0, tiled=True)  53.5 us
    psum x4, blocking collectives, feature_stats(): return lax.psum((first_part, second_part), 'col')  45.4 us
    reduce_scatter x4, waiting for transfers between devices, to_rows(): lax.psum_scatter(term(jnp.int32(0), lax.axis_size('row') * own_rows), 'ro...  45.2 us
    all_gather x2, blocking collectives, cols_in(): return lax.all_gather(block, 'col', axis=0, tiled=True)  29.8 us
    all_gather x4, blocking collectives, rows_in(): return lax.all_gather(block, 'row', axis=0, tiled=True)  23.1 us
    reduce_scatter x1, waiting for transfers between devices, local(): lax.psum_scatter(key_acc.reshape(group_rows, -1), 'col', scatter_dimensio...  22 us
  transfers between devices with their start and end apart: 13, of which 12 were waited for; matrix products, arithmetic and copies ran while one was open for 4% of the time, Pallas kernels for 0%

commit v1 on v0

--- a/solution.py
+++ b/solution.py
@@ -61,7 +61,27 @@
 
 
 def cols_in(block):
-    return lax.all_gather(block, "col", axis=0, tiled=True)
+
+    def assign_slots_by_axis(vec):
+        axis_id = "col"
+        kept_arr, part_now, frame_out = (
+            lax.axis_size(axis_id),
+            lax.axis_index(axis_id),
+            vec.shape[0],
+        )
+        arr_now = jnp.zeros((*vec.shape[:0], kept_arr * frame_out, *vec.shape[1:]), vec.dtype)
+        cards = [(pp, (pp + 1) % kept_arr) for pp in range(kept_arr)]
+        big = vec
+        dev = 0
+        while dev < kept_arr:
+            g_now = (part_now - dev) % kept_arr
+            arr_now = lax.dynamic_update_slice_in_dim(arr_now, big, g_now * frame_out, axis=0)
+            if dev < kept_arr - 1:
+                big = lax.ppermute(big, axis_name=axis_id, perm=cards)
+            dev += 1
+        return arr_now
+
+    return assign_slots_by_axis(block)
 
 
 def to_cols(whole, matrix, transposed):

time: 549 us -> 529 us (0.964)
  blocking collectives: 158 us -> 127 us
    ppermute x0 -> x12, waiting for transfers between devices: none -> 83.4 us  [assign_slots_by_axis(): big = lax.ppermute(big, axis_name=axis_id, perm=cards)]
    all_gather x2 -> x0, waiting for transfers between devices: 53.5 us -> none  [cols_in(): return lax.all_gather(block, 'col', axis=0, tiled=True)]
    all_gather x2 -> x0, blocking collectives: 29.8 us -> none  [cols_in(): return lax.all_gather(block, 'col', axis=0, tiled=True)]
    reduce_scatter x4, waiting for transfers between devices: 45.2 us -> 22.7 us  [to_rows(): lax.psum_scatter(term(jnp.int32(0), lax.axis_size('row') * own_rows), 'ro...]
  transfers between devices with their start and end apart: 13 -> 23, of which waited for: 12 -> 21; matrix products, arithmetic and copies ran while one was open for 4% -> 6% of each run, Pallas kernels for 0% -> 0%
where the time goes in v1:
time: 529 us; the launch traced here: 528 us
  waiting for transfers between devices  328 us (62%)
  blocking collectives  127 us (24%)
  matrix products  27.9 us (5%)
  other arithmetic  15.6 us (3%)
  between operations  14.5 us (3%)
  local copies, waits for them, and re-layouts  13.9 us (3%)
    reduce_scatter x4, waiting for transfers between devices, to_cols(): lax.psum_scatter(term(jnp.int32(0), lax.axis_size('col') * own_rows), 'co...  124 us
    ppermute x12, waiting for transfers between devices, assign_slots_by_axis(): big = lax.ppermute(big, axis_name=axis_id, perm=cards)  83.4 us
    psum x1, waiting for transfers between devices, local(): lax.psum((grad_qkv, grad_out, grad_up, grad_down), 'dp')  58.9 us
    psum x4, blocking collectives, feature_stats(): return lax.psum((first_part, second_part), 'col')  45.5 us
    all_gather x4, blocking collectives, rows_in(): return lax.all_gather(block, 'row', axis=0, tiled=True)  23.6 us
    reduce_scatter x4, waiting for transfers between devices, to_rows(): lax.psum_scatter(term(jnp.int32(0), lax.axis_size('row') * own_rows), 'ro...  22.7 us
    reduce_scatter x1, waiting for transfers between devices, local(): lax.psum_scatter(key_acc.reshape(group_rows, -1), 'col', scatter_dimensio...  22.1 us
    psum x1, blocking collectives, local(): lax.psum((qv_bias_part, up_bias_part), ('dp', 'col'))  18.5 us
  transfers between devices with their start and end apart: 23, of which 21 were waited for; matrix products, arithmetic and copies ran while one was open for 6% of the time, Pallas kernels for 0%

profile of v1, /device:TPU:0, one launch (start us, length us, event | category | flops | bytes accessed | tf_op | source)
XLA Modules:
  0.0 527.8 jit_solution(15325113428389233594)
XLA Ops:
  7.2 1.0 convert_reduce_fusion
  8.2 13.5 %all-reduce.5 = (f32[128]{0:T(128)S(1)}, f32[128]{0:T(128)S(1)}) all-reduce(f32[128]{0:T(128)S(1)} %get-tuple-element.85, f32[128]{0:T(128)S(1)} %get-tuple-element.84), channel_id=1, replica_groups=mesh['dp'=2,'row'=4,'col'=4] {'col'}, use_global_device_ids=true, to_apply=%region_3.0 | all-reduce | flops 256 | bytes 2048 | tf_op jit(solution)/shard_map/psum | solution.py:25
  21.7 1.0 fusion.26
  22.7 5.8 %all_gather.18 = bf16[512,256]{1,0:T(8,128)(2,1)S(1)} all-gather(bf16[128,256]{1,0:T(8,128)(2,1)S(1)} %fusion.26), channel_id=1, replica_groups=mesh['dp'=2,'row'=4,'col'=4] {'row'}, dimensions={0}, use_global_device_ids=true | all-gather | bytes 327680 | tf_op jit(solution)/shard_map/all_gather | solution.py:60
  29.2 2.5 fusion.49
  32.4 33.2 %reduce-scatter.11.cloned.1.call-done = f32[128,768]{1,0:T(8,128)} async-done(((f32[512,768]{1,0:T(8,128)}), f32[128,768]{1,0:T(8,128)}) %reduce-scatter.11.cloned.1.call-update) | async-done | bytes 393232 | tf_op jit(solution)/shard_map/reduce_scatter | solution.py:93
  65.5 1.1 copy.38
  66.9 13.4 %all_gather.19 = bf16[512,256]{0,1:T(8,128)(2,1)S(1)} all-gather(bf16[128,256]{0,1:T(8,128)(2,1)S(1)} %fusion.36), channel_id=1, replica_groups=mesh['dp'=2,'row'=4,'col'=4] {'col'}, dimensions={0}, use_global_device_ids=true | all-gather | bytes 327680 | tf_op jit(solution)/shard_map/all_gather | solution.py:156
  80.2 13.1 %all_gather.20 = bf16[512,256]{0,1:T(8,128)(2,1)S(1)} all-gather(bf16[128,256]{0,1:T(8,128)(2,1)S(1)} %bitcast.93), channel_id=1, replica_groups=mesh['dp'=2,'row'=4,'col'=4] {'col'}, dimensions={0}, use_global_device_ids=true | all-gather | bytes 327680 | tf_op jit(solution)/shard_map/all_gather | solution.py:155
  95.2 6.0 %collective-permute-done = bf16[128,256]{0,1:T(8,128)(2,1)S(1)} collective-permute-done((bf16[128,256]{0,1:T(8,128)(2,1)S(1)}, bf16[128,256]{0,1:T(8,128)(2,1)S(1)}, u32[]{:S(2)}, u32[]{:S(2)}) %collective-permute-start) | collective-permute-done | bytes 65568 | tf_op jit(solution)/shard_map/ppermute | solution.py:80
  101.2 6.0 %collective-permute-done.1 = bf16[128,256]{0,1:T(8,128)(2,1)S(1)} collective-permute-done((bf16[128,256]{0,1:T(8,128)(2,1)S(1)}, bf16[128,256]{0,1:T(8,128)(2,1)S(1)}, u32[]{:S(2)}, u32[]{:S(2)}) %collective-permute-start.1) | collective-permute-done | bytes 65568 | tf_op jit(solution)/shard_map/ppermute | solution.py:80
  107.3 6.0 %collective-permute-done.2 = bf16[128,256]{0,1:T(8,128)(2,1)S(1)} collective-permute-done((bf16[128,256]{0,1:T(8,128)(2,1)S(1)}, bf16[128,256]{0,1:T(8,128)(2,1)S(1)}, u32[]{:S(2)}, u32[]{:S(2)}) %collective-permute-start.2) | collective-permute-done | bytes 65568 | tf_op jit(solution)/shard_map/ppermute | solution.py:80
  114.0 1.1 fusion.50
  115.2 5.8 %all_gather.22 = bf16[512,256]{1,0:T(8,128)(2,1)S(1)} all-gather(bf16[128,256]{1,0:T(8,128)(2,1)S(1)} %copy-done.24), channel_id=1, replica_groups=mesh['dp'=2,'row'=4,'col'=4] {'row'}, dimensions={0}, use_global_device_ids=true | all-gather | bytes 327680 | tf_op jit(solution)/shard_map/all_gather | solution.py:60
  121.7 1.8 fusion.53
  123.6 11.4 %reduce-scatter.13.cloned.1.call-done = f32[128,256]{1,0:T(8,128)} async-done(((f32[512,256]{1,0:T(8,128)}), f32[128,256]{1,0:T(8,128)}) %reduce-scatter.13.cloned.1.call-update) | async-done | bytes 131088 | tf_op jit(solution)/shard_map/reduce_scatter | solution.py:104
  134.9 1.0 fusion.42
  136.0 11.8 %all-reduce.4 = (f32[128]{0:T(128)S(1)}, f32[128]{0:T(128)S(1)}) all-reduce(f32[128]{0:T(128)S(1)} %get-tuple-element.83, f32[128]{0:T(128)S(1)} %get-tuple-element.82), channel_id=1, replica_groups=mesh['dp'=2,'row'=4,'col'=4] {'col'}, use_global_device_ids=true, to_apply=%region_10.11 | all-reduce | flops 256 | bytes 2048 | tf_op jit(solution)/shard_map/psum | solution.py:25
  147.9 6.2 %all_gather.21 = bf16[512,256]{1,0:T(8,128)(2,1)} all-gather(bf16[128,256]{1,0:T(8,128)(2,1)S(1)} %add_convert_fusion.1), channel_id=1, replica_groups=mesh['dp'=2,'row'=4,'col'=4] {'row'}, dimensions={0}, use_global_device_ids=true | all-gather | bytes 327680 | tf_op jit(solution)/shard_map/all_gather | solution.py:60
  154.1 2.7 fusion.51
  156.9 24.0 %reduce-scatter.19.cloned.1.call-done = f32[128,1024]{1,0:T(8,128)} async-done(((f32[512,1024]{1,0:T(8,128)}), f32[128,1024]{1,0:T(8,128)}) %reduce-scatter.19.cloned.1.call-update) | async-done | bytes 524304 | tf_op jit(solution)/shard_map/reduce_scatter | solution.py:93
  180.9 44.9 %reduce-scatter.15.cloned.1.call-done = f32[128,1024]{1,0:T(8,128)} async-done(((f32[512,1024]{1,0:T(8,128)}), f32[128,1024]{1,0:T(8,128)}) %reduce-scatter.15.cloned.1.call-update) | async-done | bytes 524304 | tf_op jit(solution)/shard_map/reduce_scatter | solution.py:93
  225.8 1.6 fusion.43
  228.4 8.8 %collective-permute-done.6 = bf16[128,1024]{1,0:T(8,128)(2,1)S(1)} collective-permute-done((bf16[128,1024]{1,0:T(8,128)(2,1)S(1)}, bf16[128,1024]{1,0:T(8,128)(2,1)S(1)}, u32[]{:S(2)}, u32[]{:S(2)}) %collective-permute-start.6) | collective-permute-done | bytes 262176 | tf_op jit(solution)/shard_map/ppermute | solution.py:80
  237.2 8.6 %collective-permute-done.7 = bf16[128,1024]{1,0:T(8,128)(2,1)S(1)} collective-permute-done((bf16[128,1024]{1,0:T(8,128)(2,1)S(1)}, bf16[128,1024]{1,0:T(8,128)(2,1)S(1)}, u32[]{:S(2)}, u32[]{:S(2)}) %collective-permute-start.7) | collective-permute-done | bytes 262176 | tf_op jit(solution)/shard_map/ppermute | solution.py:80
  246.9 9.5 %collective-permute-done.8 = bf16[128,1024]{1,0:T(8,128)(2,1)S(1)} collective-permute-done((bf16[128,1024]{1,0:T(8,128)(2,1)S(1)}, bf16[128,1024]{1,0:T(8,128)(2,1)S(1)}, u32[]{:S(2)}, u32[]{:S(2)}) %collective-permute-start.8) | collective-permute-done | bytes 262176 | tf_op jit(solution)/shard_map/ppermute | solution.py:80
  256.4 1.3 fusion.54
  257.7 1.4 collective-permute-done.3
  259.2 8.2 %collective-permute-done.4 = bf16[128,1024]{1,0:T(8,128)(2,1)S(1)} collective-permute-done((bf16[128,1024]{1,0:T(8,128)(2,1)S(1)}, bf16[128,1024]{1,0:T(8,128)(2,1)S(1)}, u32[]{:S(2)}, u32[]{:S(2)}) %collective-permute-start.4) | collective-permute-done | bytes 262176 | tf_op jit(solution)/shard_map/ppermute | solution.py:80
  268.8 6.7 %collective-permute-done.5 = bf16[128,1024]{1,0:T(8,128)(2,1)S(1)} collective-permute-done((bf16[128,1024]{1,0:T(8,128)(2,1)S(1)}, bf16[128,1024]{1,0:T(8,128)(2,1)S(1)}, u32[]{:S(2)}, u32[]{:S(2)}) %collective-permute-start.5) | collective-permute-done | bytes 262176 | tf_op jit(solution)/shard_map/ppermute | solution.py:80
  276.2 2.6 fusion.52
  279.0 1.7 multiply_reduce_fusion
  280.6 10.3 %all-reduce.3 = (f32[128]{0:T(128)S(1)}, f32[128]{0:T(128)S(1)}) all-reduce(f32[128]{0:T(128)S(1)} %get-tuple-element.63, f32[128]{0:T(128)S(1)} %get-tuple-element.67), channel_id=1, replica_groups=mesh['dp'=2,'row'=4,'col'=4] {'col'}, use_global_device_ids=true, to_apply=%region_18.19 | all-reduce | flops 256 | bytes 2048 | tf_op jit(solution)/shard_map/psum | solution.py:25
  290.9 11.3 %reduce-scatter.17.cloned.1.call-done = f32[128,256]{1,0:T(8,128)} async-done(((f32[512,256]{1,0:T(8,128)}), f32[128,256]{1,0:T(8,128)}) %reduce-scatter.17.cloned.1.call-update) | async-done | bytes 131088 | tf_op jit(solution)/shard_map/reduce_scatter | solution.py:104
  302.2 2.2 fusion.45
  304.4 5.8 %all_gather.23 = bf16[512,256]{1,0:T(8,128)(2,1)S(1)} all-gather(bf16[128,256]{1,0:T(8,128)(2,1)S(1)} %convert_element_type.98), channel_id=1, replica_groups=mesh['dp'=2,'row'=4,'col'=4] {'row'}, dimensions={0}, use_global_device_ids=true | all-gather | bytes 327680 | tf_op jit(solution)/shard_map/all_gather | solution.py:60
  310.9 1.0 fusion.55
  312.0 21.9 %reduce-scatter.23.cloned.1.call-done = f32[128,256]{1,0:T(8,128)} async-done(((f32[512,256]{1,0:T(8,128)}), f32[128,256]{1,0:T(8,128)}) %reduce-scatter.23.cloned.1.call-update) | async-done | bytes 131088 | tf_op jit(solution)/shard_map/reduce_scatter | solution.py:93
  333.9 0.9 convert_element_type.99
  335.0 1.2 fusion.14
  336.7 2.0 convolution_multiply_fusion.1
  338.7 1.9 fusion.48
  340.6 16.3 %reduce-scatter.27.cloned.1.call-done = f32[128,256]{0,1:T(8,128)} async-done(((f32[512,256]{0,1:T(8,128)}), f32[128,256]{0,1:T(8,128)}) %reduce-scatter.27.cloned.1.call-update) | async-done | bytes 131088 | tf_op jit(solution)/shard_map/reduce_scatter | solution.py:239
  356.9 0.9 bitcast_convert_fusion
  357.8 22.1 %reduce-scatter.25.cloned.1.call-done = f32[128,256]{0,1:T(8,128)} async-done(((f32[512,256]{0,1:T(8,128)}), f32[128,256]{0,1:T(8,128)}) %reduce-scatter.25.cloned.1.call-update) | async-done | bytes 131088 | tf_op jit(solution)/shard_map/reduce_scatter | solution.py:238
  379.9 0.9 convert.15
  380.9 7.5 %collective-permute-done.9 = bf16[128,768]{0,1:T(8,128)(2,1)S(1)} collective-permute-done((bf16[128,768]{0,1:T(8,128)(2,1)S(1)}, bf16[128,768]{0,1:T(8,128)(2,1)S(1)}, u32[]{:S(2)}, u32[]{:S(2)}) %collective-permute-start.9) | collective-permute-done | bytes 196640 | tf_op jit(solution)/shard_map/ppermute | solution.py:80
  388.5 7.3 %collective-permute-done.10 = bf16[128,768]{0,1:T(8,128)(2,1)S(1)} collective-permute-done((bf16[128,768]{0,1:T(8,128)(2,1)S(1)}, bf16[128,768]{0,1:T(8,128)(2,1)S(1)}, u32[]{:S(2)}, u32[]{:S(2)}) %collective-permute-start.10) | collective-permute-done | bytes 196640 | tf_op jit(solution)/shard_map/ppermute | solution.py:80
  396.0 7.4 %collective-permute-done.11 = bf16[128,768]{0,1:T(8,128)(2,1)S(1)} collective-permute-done((bf16[128,768]{0,1:T(8,128)(2,1)S(1)}, bf16[128,768]{0,1:T(8,128)(2,1)S(1)}, u32[]{:S(2)}, u32[]{:S(2)}) %collective-permute-start.11) | collective-permute-done | bytes 196640 | tf_op jit(solution)/shard_map/ppermute | solution.py:80
  403.4 2.3 fusion.56
  405.8 2.4 fusion.59
  408.3 1.4 fusion.60
  409.7 0.9 fusion.58
  410.6 1.3 fusion.57
  412.3 18.5 %all-reduce = (f32[512]{0:T(512)}, f32[1024]{0:T(1024)}) all-reduce(f32[512]{0:T(512)S(1)} %reshape.258, f32[1024]{0:T(1024)S(1)} %get-tuple-element.106), channel_id=1, replica_groups=mesh['dp'=2,'row'=4,'col'=4] {'dp','col'}, use_global_device_ids=true, to_apply=%region_34.35 | all-reduce | flops 1536 | bytes 12288 | tf_op jit(solution)/shard_map/psum | solution.py:266
  430.7 1.1 fusion.31
  431.8 9.9 %all-reduce.2 = (f32[128]{0:T(128)S(1)}, f32[128]{0:T(128)S(1)}) all-reduce(f32[128]{0:T(128)S(1)} %get-tuple-element.65, f32[128]{0:T(128)S(1)} %get-tuple-element.66), channel_id=1, replica_groups=mesh['dp'=2,'row'=4,'col'=4] {'col'}, use_global_device_ids=true, to_apply=%region_27.28 | all-reduce | flops 256 | bytes 2048 | tf_op jit(solution)/shard_map/psum | solution.py:25
  441.8 13.0 %all-reduce.1 = (f32[256]{0:T(256)}, f32[256]{0:T(256)}, f32[256]{0:T(256)}, f32[256]{0:T(256)}, f32[256]{0:T(256)}, /*index=5*/f32[256]{0:T(256)}) all-reduce(f32[256]{0:T(256)S(1)} %get-tuple-element.64, f32[256]{0:T(256)S(1)} %get-tuple-element.81, f32[256]{0:T(256)S(1)} %copy-done.31, ...), channel_id=1, replica_groups=mesh['dp'=2,'row'=4,'col'=4] {'dp','row'}, use_global_device_ids=true, to_apply=%region_29.30 | all-reduce | flops 1536 | bytes 12288 | tf_op jit(solution)/shard_map/psum | solution.py:255
  454.8 1.7 fusion.30
  456.5 58.9 %all-reduce.9.cloned.1.call-done = (f32[256,768]{1,0:T(8,128)}, f32[256,256]{1,0:T(8,128)}, f32[256,1024]{1,0:T(8,128)}, f32[1024,256]{1,0:T(8,128)}) async-done(((f32[256,768]{1,0:T(8,128)}, f32[256,256]{1,0:T(8,128)}, f32[256,1024]{1,0:T(8,128)}, f32[1024,256]{1,0:T(8,128)}), (f32[256,768]{1,0:T(8,128)}, f32[256,256]{1,0:T(8,128)}, f32[256,1024]{1,0:T(8,128)}, ...) | async-done | bytes 3145744 | tf_op jit(solution)/shard_map/psum | solution.py:252
  515.4 2.2 copy.62
  517.6 1.7 copy.63
  519.3 1.0 copy.64
  520.3 1.0 copy.65
  (160 shorter events, 11.4 us)
Async XLA Ops:
  7.2 147.0 %copy-start = (bf16[256,1024]{1,0:T(8,128)(2,1)S(1)}, bf16[256,1024]{1,0:T(8,128)(2,1)}, u32[]{:S(2)}) copy-start(bf16[256,1024]{1,0:T(8,128)(2,1)} %param.24) | copy-start | bytes 1572868
  7.2 58.3 %reduce-scatter.11.cloned.1.call-start = ((), (), s32[]{:S(2)}) async-start(), calls=%async_computation.10 | async-start | bytes 1966080 | tf_op jit(solution)/shard_map/reduce_scatter | solution.py:93
  22.7 9.2 %copy-start.33 = (f32[512]{0:T(512)S(1)}, f32[512]{0:T(512)}, u32[]{:S(2)}) copy-start(f32[512]{0:T(512)} %param.19) | copy-start | bytes 6148
  28.5 0.7 copy-start.3
  31.7 103.2 %reduce-scatter.13.cloned.1.call-start = ((), (), s32[]{:S(2)}) async-start(), calls=%async_computation.11 | async-start | bytes 655360 | tf_op jit(solution)/shard_map/reduce_scatter | solution.py:104
  32.0 62.7 %copy-start.28 = (f32[4,1,64]{2,1,0:T(1,128)}, f32[4,1,64]{2,1,0:T(1,128)S(1)}, u32[]{:S(2)}) copy-start(f32[4,1,64]{2,1,0:T(1,128)S(1)} %get-tuple-element.117) | copy-start | bytes 3076
  66.7 26.7 %copy-start.14 = (f32[128,768]{0,1:T(8,128)}, f32[128,768]{0,1:T(8,128)S(1)}, u32[]{:S(2)}) copy-start(f32[128,768]{0,1:T(8,128)S(1)} %copy.38) | copy-start | bytes 1179652
  93.4 0.7 copy-start.19
  94.0 20.0 %copy-start.20 = (bf16[256,256]{1,0:T(8,128)(2,1)S(1)}, bf16[256,256]{1,0:T(8,128)(2,1)}, u32[]{:S(2)}) copy-start(bf16[256,256]{1,0:T(8,128)(2,1)} %param.20) | copy-start | bytes 393220
  94.7 20.4 %copy-start.24 = (bf16[128,256]{1,0:T(8,128)(2,1)S(1)}, bf16[128,256]{1,0:T(8,128)(2,1)}, u32[]{:S(2)}) copy-start(bf16[128,256]{1,0:T(8,128)(2,1)} %param.15) | copy-start | bytes 196612
  94.7 26.9 %copy-start.12 = (bf16[1024,256]{1,0:T(8,128)(2,1)S(1)}, bf16[1024,256]{1,0:T(8,128)(2,1)}, u32[]{:S(2)}) copy-start(bf16[1024,256]{1,0:T(8,128)(2,1)} %param.26) | copy-start | bytes 1572868
  95.1 6.1 %collective-permute-start = (bf16[128,256]{0,1:T(8,128)(2,1)S(1)}, bf16[128,256]{0,1:T(8,128)(2,1)S(1)}, u32[]{:S(2)}, u32[]{:S(2)}) collective-permute-start(bf16[128,256]{0,1:T(8,128)(2,1)S(1)} %bitcast.90), channel_id=1, source_target_pairs={{0,1},{1,2},{2,3},{3,0},{4,5},{5,6},{6,7},{7,4},{8,9},{9,10},{10,1... | collective-permute-start | bytes 196616 | tf_op jit(solution)/shard_map/ppermute | solution.py:80
  101.2 6.1 %collective-permute-start.1 = (bf16[128,256]{0,1:T(8,128)(2,1)S(1)}, bf16[128,256]{0,1:T(8,128)(2,1)S(1)}, u32[]{:S(2)}, u32[]{:S(2)}) collective-permute-start(bf16[128,256]{0,1:T(8,128)(2,1)S(1)} %collective-permute-done), channel_id=1, source_target_pairs={{0,1},{1,2},{2,3},{3,0},{4,5},{5,6},{6,7},{7,4},{8,9},{9,10},{10,1... | collective-permute-start | bytes 196616 | tf_op jit(solution)/shard_map/ppermute | solution.py:80
  107.2 6.1 %collective-permute-start.2 = (bf16[128,256]{0,1:T(8,128)(2,1)S(1)}, bf16[128,256]{0,1:T(8,128)(2,1)S(1)}, u32[]{:S(2)}, u32[]{:S(2)}) collective-permute-start(bf16[128,256]{0,1:T(8,128)(2,1)S(1)} %collective-permute-done.1), channel_id=1, source_target_pairs={{0,1},{1,2},{2,3},{3,0},{4,5},{5,6},{6,7},{7,4},{8,9},{9,10},{10,1... | collective-permute-start | bytes 196616 | tf_op jit(solution)/shard_map/ppermute | solution.py:80
  113.3 0.7 copy-start.7
  115.1 65.8 %reduce-scatter.19.cloned.1.call-start = ((), (), s32[]{:S(2)}) async-start(), calls=%async_computation.14 | async-start | bytes 2621440 | tf_op jit(solution)/shard_map/reduce_scatter | solution.py:93
  120.9 0.7 copy-start.9
  121.6 13.3 %copy-start.13 = (bf16[128,256]{1,0:T(8,128)(2,1)S(1)}, bf16[128,256]{1,0:T(8,128)(2,1)}, u32[]{:S(2)}) copy-start(bf16[128,256]{1,0:T(8,128)(2,1)} %param.14) | copy-start | bytes 196612
  121.6 13.3 %copy-start.34 = (f32[256]{0:T(256)S(1)}, f32[256]{0:T(256)}, u32[]{:S(2)}) copy-start(f32[256]{0:T(256)} %param.21) | copy-start | bytes 3076
  121.6 26.1 %copy-start.26 = (f32[256]{0:T(256)S(1)}, f32[256]{0:T(256)}, u32[]{:S(2)}) copy-start(f32[256]{0:T(256)} %param.22) | copy-start | bytes 3076
  121.7 26.1 %copy-start.35 = (f32[256]{0:T(256)S(1)}, f32[256]{0:T(256)}, u32[]{:S(2)}) copy-start(f32[256]{0:T(256)} %param.23) | copy-start | bytes 3076
  123.5 102.3 %reduce-scatter.15.cloned.1.call-start = ((), (), s32[]{:S(2)}) async-start(), calls=%async_computation.12 | async-start | bytes 2621440 | tf_op jit(solution)/shard_map/reduce_scatter | solution.py:93
  154.1 71.7 %copy-start.25 = (f32[1024]{0:T(1024)S(1)}, f32[1024]{0:T(1024)}, u32[]{:S(2)}) copy-start(f32[1024]{0:T(1024)} %param.25) | copy-start | bytes 12292
  156.9 122.1 %reduce-scatter.21.cloned.1.call-start = ((), (), s32[]{:S(2)}) async-start(), calls=%async_computation.15 | async-start | bytes 655360 | tf_op jit(solution)/shard_map/reduce_scatter | solution.py:104
  225.8 20.1 %copy-start.11 = (f32[128,1024]{1,0:T(8,128)S(1)}, f32[128,1024]{1,0:T(8,128)}, u32[]{:S(2)}) copy-start(f32[128,1024]{1,0:T(8,128)} %reduce-scatter.15.cloned.1.call-done) | copy-start | bytes 1572868
  227.7 9.5 %collective-permute-start.6 = (bf16[128,1024]{1,0:T(8,128)(2,1)S(1)}, bf16[128,1024]{1,0:T(8,128)(2,1)S(1)}, u32[]{:S(2)}, u32[]{:S(2)}) collective-permute-start(bf16[128,1024]{1,0:T(8,128)(2,1)S(1)} %get-tuple-element.111), channel_id=1, source_target_pairs={{0,1},{1,2},{2,3},{3,0},{4,5},{5,6},{6,7},{7,4},{8,9},{9,10},{10,1... | collective-permute-start | bytes 786440 | tf_op jit(solution)/shard_map/ppermute | solution.py:80
  237.2 8.6 %collective-permute-start.7 = (bf16[128,1024]{1,0:T(8,128)(2,1)S(1)}, bf16[128,1024]{1,0:T(8,128)(2,1)S(1)}, u32[]{:S(2)}, u32[]{:S(2)}) collective-permute-start(bf16[128,1024]{1,0:T(8,128)(2,1)S(1)} %collective-permute-done.6), channel_id=1, source_target_pairs={{0,1},{1,2},{2,3},{3,0},{4,5},{5,6},{6,7},{7,4},{8,9},{9,10},{10,1... | collective-permute-start | bytes 786440 | tf_op jit(solution)/shard_map/ppermute | solution.py:80
  245.8 10.6 %collective-permute-start.8 = (bf16[128,1024]{1,0:T(8,128)(2,1)S(1)}, bf16[128,1024]{1,0:T(8,128)(2,1)S(1)}, u32[]{:S(2)}, u32[]{:S(2)}) collective-permute-start(bf16[128,1024]{1,0:T(8,128)(2,1)S(1)} %collective-permute-done.7), channel_id=1, source_target_pairs={{0,1},{1,2},{2,3},{3,0},{4,5},{5,6},{6,7},{7,4},{8,9},{9,10},{10,1... | collective-permute-start | bytes 786440 | tf_op jit(solution)/shard_map/ppermute | solution.py:80
  246.8 9.6 %copy-start.1 = (bf16[512,1024]{1,0:T(8,128)(2,1)}, bf16[512,1024]{1,0:T(8,128)(2,1)S(1)}, u32[]{:S(2)}) copy-start(bf16[512,1024]{1,0:T(8,128)(2,1)S(1)} %get-tuple-element.112) | copy-start | bytes 3145732
  246.8 12.3 %collective-permute-start.3 = (bf16[128,1024]{1,0:T(8,128)(2,1)}, bf16[128,1024]{1,0:T(8,128)(2,1)S(1)}, u32[]{:S(2)}, u32[]{:S(2)}) collective-permute-start(bf16[128,1024]{1,0:T(8,128)(2,1)} %get-tuple-element.113), channel_id=1, source_target_pairs={{0,1},{1,2},{2,3},{3,0},{4,5},{5,6},{6,7},{7,4},{8,9},{9,10},{10,1... | collective-permute-start | bytes 786440 | tf_op jit(solution)/shard_map/ppermute | solution.py:80
  257.7 44.5 %reduce-scatter.17.cloned.1.call-start = ((), (), s32[]{:S(2)}) async-start(), calls=%async_computation.13 | async-start | bytes 655360 | tf_op jit(solution)/shard_map/reduce_scatter | solution.py:104
  259.1 8.2 %collective-permute-start.4 = (bf16[128,1024]{1,0:T(8,128)(2,1)S(1)}, bf16[128,1024]{1,0:T(8,128)(2,1)S(1)}, u32[]{:S(2)}, u32[]{:S(2)}) collective-permute-start(bf16[128,1024]{1,0:T(8,128)(2,1)S(1)} %collective-permute-done.3), channel_id=1, source_target_pairs={{0,1},{1,2},{2,3},{3,0},{4,5},{5,6},{6,7},{7,4},{8,9},{9,10},{10,1... | collective-permute-start | bytes 786440 | tf_op jit(solution)/shard_map/ppermute | solution.py:80
  267.3 8.2 %collective-permute-start.5 = (bf16[128,1024]{1,0:T(8,128)(2,1)S(1)}, bf16[128,1024]{1,0:T(8,128)(2,1)S(1)}, u32[]{:S(2)}, u32[]{:S(2)}) collective-permute-start(bf16[128,1024]{1,0:T(8,128)(2,1)S(1)} %collective-permute-done.4), channel_id=1, source_target_pairs={{0,1},{1,2},{2,3},{3,0},{4,5},{5,6},{6,7},{7,4},{8,9},{9,10},{10,1... | collective-permute-start | bytes 786440 | tf_op jit(solution)/shard_map/ppermute | solution.py:80
  268.0 34.1 %copy-start.36 = (f32[256]{0:T(256)S(1)}, f32[256]{0:T(256)}, u32[]{:S(2)}) copy-start(f32[256]{0:T(256)} %param.27) | copy-start | bytes 3076
  276.2 34.6 %copy-start.21 = (bf16[256,256]{1,0:T(8,128)(2,1)S(1)}, bf16[256,256]{1,0:T(8,128)(2,1)}, u32[]{:S(2)}) copy-start(bf16[256,256]{1,0:T(8,128)(2,1)} %param.20) | copy-start | bytes 393220
  278.9 55.0 %reduce-scatter.23.cloned.1.call-start = ((), (), s32[]{:S(2)}) async-start(), calls=%async_computation.16 | async-start | bytes 655360 | tf_op jit(solution)/shard_map/reduce_scatter | solution.py:93
  304.4 31.8 %copy-start.15 = (f32[128,256]{1,0:T(8,128)}, f32[128,256]{1,0:T(8,128)S(1)}, u32[]{:S(2)}) copy-start(f32[128,256]{1,0:T(8,128)S(1)} %get-tuple-element.109) | copy-start | bytes 393220
  310.1 0.7 copy-start.5
  311.9 45.0 %reduce-scatter.27.cloned.1.call-start = ((), (), s32[]{:S(2)}) async-start(), calls=%async_computation.18 | async-start | bytes 655360 | tf_op jit(solution)/shard_map/reduce_scatter | solution.py:239
  336.2 43.7 %reduce-scatter.25.cloned.1.call-start = ((), (), s32[]{:S(2)}) async-start(), calls=%async_computation.17 | async-start | bytes 655360 | tf_op jit(solution)/shard_map/reduce_scatter | solution.py:238
  338.7 92.1 %reduce-scatter.29.cloned.1.call-start = ((), (), s32[]{:S(2)}) async-start(), calls=%async_computation.19 | async-start | bytes 655360 | tf_op jit(solution)/shard_map/reduce_scatter | solution.py:104
  380.9 7.5 %collective-permute-start.9 = (bf16[128,768]{0,1:T(8,128)(2,1)S(1)}, bf16[128,768]{0,1:T(8,128)(2,1)S(1)}, u32[]{:S(2)}, u32[]{:S(2)}) collective-permute-start(bf16[128,768]{0,1:T(8,128)(2,1)S(1)} %bitcast.88), channel_id=1, source_target_pairs={{0,1},{1,2},{2,3},{3,0},{4,5},{5,6},{6,7},{7,4},{8,9},{9,10},{10,1... | collective-permute-start | bytes 589832 | tf_op jit(solution)/shard_map/ppermute | solution.py:80
  388.4 7.5 %collective-permute-start.10 = (bf16[128,768]{0,1:T(8,128)(2,1)S(1)}, bf16[128,768]{0,1:T(8,128)(2,1)S(1)}, u32[]{:S(2)}, u32[]{:S(2)}) collective-permute-start(bf16[128,768]{0,1:T(8,128)(2,1)S(1)} %collective-permute-done.9), channel_id=1, source_target_pairs={{0,1},{1,2},{2,3},{3,0},{4,5},{5,6},{6,7},{7,4},{8,9},{9,10},{10,1... | collective-permute-start | bytes 589832 | tf_op jit(solution)/shard_map/ppermute | solution.py:80
  395.8 7.5 %collective-permute-start.11 = (bf16[128,768]{0,1:T(8,128)(2,1)S(1)}, bf16[128,768]{0,1:T(8,128)(2,1)S(1)}, u32[]{:S(2)}, u32[]{:S(2)}) collective-permute-start(bf16[128,768]{0,1:T(8,128)(2,1)S(1)} %collective-permute-done.10), channel_id=1, source_target_pairs={{0,1},{1,2},{2,3},{3,0},{4,5},{5,6},{6,7},{7,4},{8,9},{9,10},{10,1... | collective-permute-start | bytes 589832 | tf_op jit(solution)/shard_map/ppermute | solution.py:80
  403.4 4.9 copy-start.2
  405.7 109.7 %all-reduce.9.cloned.1.call-start = ((), (), s32[]{:S(2)}) async-start(), calls=%async_computation.20 | async-start | bytes 6291456 | tf_op jit(solution)/shard_map/psum | solution.py:252
  405.8 2.5 copy-start.10
  405.8 3.9 copy-start.6
  405.8 3.9 copy-start.8
  408.3 2.4 copy-start.4
  410.6 1.4 copy-start.22
  410.6 1.4 copy-start.23
  411.9 18.8 %copy-start.27 = (f32[256]{0:T(256)S(1)}, f32[256]{0:T(256)}, u32[]{:S(2)}) copy-start(f32[256]{0:T(256)} %param.16) | copy-start | bytes 3076
  411.9 29.8 %copy-start.29 = (f32[256]{0:T(256)S(1)}, f32[256]{0:T(256)}, u32[]{:S(2)}) copy-start(f32[256]{0:T(256)} %get-tuple-element.62) | copy-start | bytes 3076
  411.9 29.8 %copy-start.30 = (f32[256]{0:T(256)S(1)}, f32[256]{0:T(256)}, u32[]{:S(2)}) copy-start(f32[256]{0:T(256)} %get-tuple-element.80) | copy-start | bytes 3076
  411.9 29.8 %copy-start.31 = (f32[256]{0:T(256)S(1)}, f32[256]{0:T(256)}, u32[]{:S(2)}) copy-start(f32[256]{0:T(256)} %get-tuple-element.108) | copy-start | bytes 3076
  411.9 29.8 %copy-start.32 = (f32[256]{0:T(256)S(1)}, f32[256]{0:T(256)}, u32[]{:S(2)}) copy-start(f32[256]{0:T(256)} %get-tuple-element.116) | copy-start | bytes 3076
  412.0 42.8 %copy-start.16 = (f32[128,256]{1,0:T(8,128)S(1)}, f32[128,256]{1,0:T(8,128)}, u32[]{:S(2)}) copy-start(f32[128,256]{1,0:T(8,128)} %copy-done.15) | copy-start | bytes 393220
  515.4 3.9 copy-start.18
  515.4 4.9 copy-start.17
Sparse Core Ops, SparseCore 0:
  31.9 33.6 reduce-scatter.10
  115.2 19.6 reduce-scatter.12
  137.2 43.6 reduce-scatter.18
  183.1 42.7 reduce-scatter.14
  257.8 19.7 reduce-scatter.20
  280.5 21.6 reduce-scatter.16
  312.0 21.8 reduce-scatter.22
  336.8 20.1 reduce-scatter.26
  359.8 20.0 reduce-scatter.24
  405.8 19.7 reduce-scatter.28
  429.2 86.1 all-reduce.8
